TPU v7x, 256 devices: a whole 4x4x8 slice. The times are simulated.
256 devices in a mesh: tm: 8 (over z), height: 16 (over x, y), cam: 2 (over core).
Axes of the slice: x: 4, y: 4, z: 8, core: 2. Of those that a mesh axis runs over, the one named last changes fastest.
Arguments:
- video_clip: bfloat16 [2, 32, 128, 64, 256], P('cam', 'tm', 'height'), may hold values from -6 to 6
- valid_from: int32 [2], P('cam'), may hold values from 0 to 16, as said below
- norm_gain: float32 [256], replicated, may hold values from 0.5 to 1.5
- spatial_weight: bfloat16 [3, 3, 256, 256], replicated, may hold values from -0.125 to 0.125
- temporal_weight: bfloat16 [3, 256, 256], replicated, may hold values from -0.21875 to 0.21875
- mix_weight: bfloat16 [3, 256, 256], replicated, may hold values from -0.21875 to 0.21875
- cotangent: bfloat16 [2, 16, 128, 64, 256], P('cam', None, ('height', 'tm')), may hold values from -6 to 6
Outputs:
- encoded: bfloat16 [2, 16, 128, 64, 256], P('cam', None, ('height', 'tm'))
- video_gradient: bfloat16 [2, 32, 128, 64, 256], P('cam', 'tm', 'height')
- spatial_gradient: float32 [3, 3, 256, 256], replicated
- temporal_gradient: float32 [3, 256, 256], replicated
- mix_gradient: float32 [3, 256, 256], replicated
- gain_gradient: float32 [256], replicated
Inputs may be any that keep to these rules, and one draw needn't show every extreme that they name: Frames before valid_from of a camera are padding. In every draw some camera starts at 16.
All inputs are finite; a program needn't handle non-finite values.
Results may differ from a plain program's by a relative error of at most 0.0065.
Values may be sent and summed in bfloat16 or wider, within the bound.
A program may use at most 128 MiB of HBM per device.

v0:
```python
import math
import jax
import jax.numpy as jnp
from jax import lax
from jax.sharding import PartitionSpec as P


def extended(array, sides, width):
    for axis, dim in sides:
        size, length = (lax.axis_size(axis), array.shape[dim])
        up = [(i, (i + 1) % size) for i in range(size - 1)]
        down = [(j, i) for i, j in up]
        last = lax.slice_in_dim(array, length - width, length, axis=dim)
        initial = lax.slice_in_dim(array, 0, width, axis=dim)
        before = lax.ppermute(last, axis, up)
        after = lax.ppermute(initial, axis, down)
        array = jnp.concatenate([before, array, after], axis=dim)
    return array


def shifted(block, axis, distance):
    devices = range(lax.axis_size(axis))
    route = [(i - distance, i) for i in devices if i - distance in devices]
    return lax.ppermute(block, axis, route)


def project(rows_in, weight):
    flat_rows = rows_in.reshape(-1, rows_in.shape[-1])
    product = jnp.dot(flat_rows, weight, preferred_element_type=jnp.float32)
    return product.reshape(rows_in.shape[:-1] + (weight.shape[-1],))


def project_back(rows_in, weight):
    flat_rows = rows_in.reshape(-1, rows_in.shape[-1])
    product = lax.dot_general(
        flat_rows, weight, (((1,), (1,)), ((), ())), preferred_element_type=jnp.float32
    )
    return product.reshape(rows_in.shape[:-1] + (weight.shape[0],))


def outer_sum(left_rows, right_rows):
    return lax.dot_general(
        left_rows.reshape(-1, left_rows.shape[-1]),
        right_rows.reshape(-1, right_rows.shape[-1]),
        (((0,), (0,)), ((), ())),
        preferred_element_type=jnp.float32,
    )


def column_pad(padded):
    return jnp.pad(padded, ((0, 0), (0, 0), (0, 0), (1, 1), (0, 0)))


def spatial(padded, weight):
    columns = column_pad(padded)
    rows_here = padded.shape[2] - 2
    width_here = padded.shape[3]
    accumulated = jnp.zeros(
        padded.shape[:2] + (rows_here, width_here, weight.shape[-1]), jnp.float32
    )
    for row_tap in range(3):
        for column_tap in range(3):
            window = columns[
                :, :, row_tap : row_tap + rows_here, column_tap : column_tap + width_here
            ]
            accumulated = accumulated + project(window, weight[row_tap, column_tap])
    return accumulated


def spatial_grad(padded, gradient):
    columns = column_pad(padded)
    rows_here = padded.shape[2] - 2
    width_here = padded.shape[3]
    outer_rows = []
    for row_tap in range(3):
        inner_rows = []
        for column_tap in range(3):
            window = columns[
                :, :, row_tap : row_tap + rows_here, column_tap : column_tap + width_here
            ]
            inner_rows.append(outer_sum(window, gradient))
        outer_rows.append(jnp.stack(inner_rows))
    return jnp.stack(outer_rows)


def flipped(weight):
    return jnp.transpose(weight[::-1, ::-1], (0, 1, 3, 2))


def norm_forward(masked, norm_gain):
    values = masked.astype(jnp.float32)
    inverse = lax.rsqrt(jnp.mean(values * values, axis=-1, keepdims=True) + 1e-06)
    unit_rows = values * inverse
    return ((unit_rows * norm_gain).astype(jnp.bfloat16), unit_rows, inverse)


def norm_backward(normed_gradient, unit_rows, inverse, norm_gain, present):
    unit_gradient = normed_gradient * norm_gain
    masked_gradient = inverse * (
        unit_gradient - unit_rows * jnp.mean(unit_gradient * unit_rows, axis=-1, keepdims=True)
    )
    video_gradient = jnp.where(present, masked_gradient, jnp.zeros_like(masked_gradient)).astype(
        jnp.bfloat16
    )
    gain_gradient = jnp.sum((normed_gradient * unit_rows).reshape(-1, unit_rows.shape[-1]), axis=0)
    return (video_gradient, gain_gradient)


def split_frames(active, prior_frame):
    dims_in = active.shape
    frame_pairs = active.reshape(dims_in[0], dims_in[1] // 2, 2, dims_in[2], dims_in[3], dims_in[4])
    even_frames = frame_pairs[:, :, 0]
    odd_frames = frame_pairs[:, :, 1]
    prior_odd = jnp.concatenate([prior_frame, odd_frames[:, :-1]], axis=1)
    return (even_frames, odd_frames, prior_odd)


def temporal_forward(even_frames, odd_frames, prior_odd, weight):
    accumulated = (
        project(odd_frames, weight[0])
        + project(even_frames, weight[1])
        + project(prior_odd, weight[2])
    )
    return accumulated.astype(jnp.bfloat16)


def temporal_backward(even_frames, odd_frames, prior_odd, strided_gradient, following, weight):
    weight_gradient = jnp.stack(
        [
            outer_sum(odd_frames, strided_gradient),
            outer_sum(even_frames, strided_gradient),
            outer_sum(prior_odd, strided_gradient),
        ]
    )
    next_gradient = jnp.concatenate([strided_gradient[:, 1:], following], axis=1)
    odd_gradient = project_back(strided_gradient, weight[0]) + project_back(
        next_gradient, weight[2]
    )
    even_gradient = project_back(strided_gradient, weight[1])
    dims_in = even_frames.shape
    active_gradient = jnp.stack([even_gradient, odd_gradient], axis=2).reshape(
        dims_in[0], dims_in[1] * 2, dims_in[2], dims_in[3], dims_in[4]
    )
    return (active_gradient, weight_gradient)


def mix_forward(regrouped, weight):
    frame_count = regrouped.shape[1]
    blank_frames = jnp.zeros(regrouped.shape[:1] + (2,) + regrouped.shape[2:], regrouped.dtype)
    history = jnp.concatenate([blank_frames, regrouped], axis=1)
    accumulated = regrouped.astype(jnp.float32)
    for offset in range(3):
        accumulated = accumulated + project(
            history[:, 2 - offset : 2 - offset + frame_count], weight[offset]
        )
    return (accumulated.astype(jnp.bfloat16), history)


def mix_backward(history, cotangent, weight):
    frame_count = cotangent.shape[1]
    mix_gradient = jnp.stack(
        [
            outer_sum(history[:, 2 - offset : 2 - offset + frame_count], cotangent)
            for offset in range(3)
        ]
    )
    blank_frames = jnp.zeros(cotangent.shape[:1] + (2,) + cotangent.shape[2:], cotangent.dtype)
    ahead = jnp.concatenate([cotangent, blank_frames], axis=1)
    accumulated = cotangent.astype(jnp.float32)
    for offset in range(3):
        accumulated = accumulated + project_back(
            ahead[:, offset : offset + frame_count], weight[offset]
        )
    return (mix_gradient, accumulated.astype(jnp.bfloat16))


def activation_backward(active_gradient, pre_activation):
    sigmoid_value = jax.nn.sigmoid(pre_activation)
    return (
        active_gradient * sigmoid_value * (1.0 + pre_activation * (1.0 - sigmoid_value))
    ).astype(jnp.bfloat16)


def on_device(
    video_clip, valid_from, norm_gain, spatial_weight, temporal_weight, mix_weight, cotangent
):
    frames_here = video_clip.shape[1]
    frames = lax.axis_index("tm") * frames_here + jnp.arange(frames_here, dtype=jnp.int32)
    present = (frames[None, :] >= valid_from[:, None])[:, :, None, None, None]
    masked = jnp.where(present, video_clip, jnp.zeros_like(video_clip))
    normed, unit_rows, inverse = norm_forward(masked, norm_gain)
    padded = extended(normed, (("height", 2),), 1)
    pre_activation = spatial(padded, spatial_weight)
    active = jax.nn.silu(pre_activation).astype(jnp.bfloat16)
    prior_frame = shifted(active[:, frames_here - 1 :], "tm", 1)
    even_frames, odd_frames, prior_odd = split_frames(active, prior_frame)
    strided = temporal_forward(even_frames, odd_frames, prior_odd, temporal_weight)
    regrouped = lax.all_to_all(strided, "tm", split_axis=2, concat_axis=1, tiled=True)
    encoded, history = mix_forward(regrouped, mix_weight)
    mix_gradient, regrouped_gradient = mix_backward(history, cotangent, mix_weight)
    strided_gradient = lax.all_to_all(
        regrouped_gradient, "tm", split_axis=1, concat_axis=2, tiled=True
    )
    following = shifted(strided_gradient[:, :1], "tm", -1)
    active_gradient, temporal_gradient = temporal_backward(
        even_frames, odd_frames, prior_odd, strided_gradient, following, temporal_weight
    )
    pre_gradient = activation_backward(active_gradient, pre_activation)
    spatial_gradient = spatial_grad(padded, pre_gradient)
    gradient_padded = extended(pre_gradient, (("height", 2),), 1)
    normed_gradient = spatial(gradient_padded, flipped(spatial_weight))
    video_gradient, gain_gradient = norm_backward(
        normed_gradient, unit_rows, inverse, norm_gain, present
    )
    mix_gradient, temporal_gradient, spatial_gradient, gain_gradient = lax.psum(
        (mix_gradient, temporal_gradient, spatial_gradient, gain_gradient), ("tm", "height", "cam")
    )
    cell_count = (
        video_clip.shape[0]
        * lax.axis_size("cam")
        * frames_here
        * lax.axis_size("tm")
        * video_clip.shape[2]
        * lax.axis_size("height")
        * video_clip.shape[3]
    )
    gradient_scale = 1.0 / math.sqrt(cell_count)
    return (
        encoded,
        video_gradient,
        spatial_gradient * gradient_scale,
        temporal_gradient * gradient_scale,
        mix_gradient * gradient_scale,
        gain_gradient * gradient_scale,
    )


def solution(mesh):
    return jax.shard_map(
        on_device,
        mesh=mesh,
        in_specs=(
            P("cam", "tm", "height", None, None),
            P("cam"),
            P(),
            P(),
            P(),
            P(),
            P("cam", None, ("height", "tm"), None, None),
        ),
        out_specs=(
            P("cam", None, ("height", "tm"), None, None),
            P("cam", "tm", "height", None, None),
            P(),
            P(),
            P(),
            P(),
        ),
        check_vma=False,
    )
```

profile of v0, /device:TPU:2, one launch (start us, length us, event | category | flops | bytes accessed | tf_op | source)
XLA Modules:
  0.0 402.6 jit_solution(15002015680635062406)
XLA Ops:
  12.0 3.5 collective-permute-start
  15.5 4.5 %collective-permute-start.1 = (bf16[1,4,1,64,256]{4,3,2,1,0:T(8,128)(2,1)}, bf16[1,4,1,64,256]{4,3,2,1,0:T(8,128)(2,1)S(1)}, u32[]{:S(2)}, u32[]{:S(2)}) collective-permute-start(bf16[1,4,1,64,256]{4,3,2,1,0:T(8,128)(2,1)} %get-tuple-element.43), channel_id=1, source_target_pairs={{2,0},{4,2},{6,4},{8,6},{10,8},{12,10},{14,12},{16,14},{18,16},{20... | collective-permute-start | bytes 393224 | tf_op jit(solution)/shard_map/ppermute | solution.py:16
  21.8 8.5 %all-to-all-start.1 = ((bf16[1,16,1,64,256]{4,3,2,0,1:T(8,128)(2,1)}), bf16[1,16,1,64,256]{4,3,2,0,1:T(8,128)(2,1)S(1)}, u32[]{:S(2)}, u32[]{:S(2)}) async-start(bf16[1,16,1,64,256]{4,3,2,0,1:T(8,128)(2,1)} %fusion.23), calls=%async_computation.1 | async-start | bytes 1048576 | tf_op jit(solution)/shard_map/all_to_all | solution.py:201
  30.3 1.8 fusion.42
  33.6 2.5 reverse_bitcast_fusion
  36.9 1.8 fusion.44
  38.7 1.8 fusion.45
  40.5 1.8 fusion.46
  42.3 1.9 fusion.51
  44.2 1.8 fusion.47
  47.7 1.8 fusion.49
  53.6 7.1 %collective-permute-done.3 = bf16[1,1,8,64,256]{4,3,2,1,0:T(8,128)(2,1)S(1)} collective-permute-done((bf16[1,1,8,64,256]{4,3,2,1,0:T(8,128)(2,1)S(1)}, bf16[1,1,8,64,256]{4,3,2,1,0:T(8,128)(2,1)S(1)}, u32[]{:S(2)}, u32[]{:S(2)}) %collective-permute-start.3) | collective-permute-done | bytes 262176 | tf_op jit(solution)/shard_map/ppermute | solution.py:24
  64.6 3.2 fusion.14
  71.9 3.8 collective-permute-start.2
  76.0 1.9 collective-permute-start.4
  77.9 6.2 %collective-permute-start.5 = (bf16[1,4,1,64,256]{4,3,2,1,0:T(8,128)(2,1)S(1)}, bf16[1,4,1,64,256]{4,3,2,1,0:T(8,128)(2,1)S(1)}, u32[]{:S(2)}, u32[]{:S(2)}) collective-permute-start(bf16[1,4,1,64,256]{4,3,2,1,0:T(8,128)(2,1)S(1)} %get-tuple-element.41), channel_id=1, source_target_pairs={{2,0},{4,2},{6,4},{8,6},{10,8},{12,10},{14,12},{16,14},{18,16},{20... | collective-permute-start | bytes 393224 | tf_op jit(solution)/shard_map/ppermute | solution.py:16
  84.1 1.8 fusion.77
  91.9 1.8 fusion.26
  93.7 1.8 fusion.30
  95.5 1.8 fusion.31
  97.3 1.7 fusion.32
  100.6 5.8 %all-to-all-start = ((bf16[1,2,8,64,256]{4,3,1,0,2:T(8,128)(2,1)}), bf16[1,2,8,64,256]{4,3,1,0,2:T(8,128)(2,1)}, u32[]{:S(2)}, u32[]{:S(2)}) async-start(bf16[1,2,8,64,256]{4,3,1,0,2:T(8,128)(2,1)} %copy.41), calls=%async_computation | async-start | bytes 1048576 | tf_op jit(solution)/shard_map/all_to_all | solution.py:198
  106.5 2.8 fusion.35
  109.3 2.7 fusion.33
  111.9 2.7 fusion.38
  115.0 6.2 %all-to-all-done = bf16[1,2,8,64,256]{4,3,1,0,2:T(8,128)(2,1)} async-done(((bf16[1,2,8,64,256]{4,3,1,0,2:T(8,128)(2,1)}), bf16[1,2,8,64,256]{4,3,1,0,2:T(8,128)(2,1)}, u32[]{:S(2)}, u32[]{:S(2)}) %all-to-all-start) | async-done | bytes 524320 | tf_op jit(solution)/shard_map/all_to_all | solution.py:198
  127.9 7.8 %fusion.11 = (f32[256]{0:T(256)S(1)}, f32[4,8,64]{2,1,0:T(8,128)S(1)}, f32[4,8,64,256]{3,2,1,0:T(8,128)}) fusion(f32[4,8,64]{2,1,0:T(8,128)S(1)} %add_rsqrt_fusion, bf16[1,4,8,64,256]{4,3,2,1,0:T(8,128)(2,1)S(1)} %copy-done.2, pred[4]{0:T(512)(128)(4,1)S(1)} %add_compare_fusion, f32[256]{0:T(256)S(1)} %copy-done.32, f32[4,8,64,256]{3,2,1,0:T(8,128)} %fusion.26, ...), kind=kOutput, calls=%fused_computation.16 | convolution fusion | flops 277346048 | bytes 21252100 | tf_op jit(solution)/shard_map/dot_general | solution.py:29
  135.7 71.9 %psum.31 = f32[256]{0:T(256)S(1)} all-reduce(f32[256]{0:T(256)S(1)} %get-tuple-element.30), channel_id=1, replica_groups=mesh['tm'=8,'height'=16,'cam'=2] {'tm','height','cam'}, use_global_device_ids=true, to_apply=%region_6.7 | all-reduce | flops 256 | bytes 2048 | tf_op jit(solution)/shard_map/psum | solution.py:215
  208.2 2.9 fusion.10
  213.9 2.1 fusion.24
  216.0 174.5 %all-reduce.7.cloned.1.call-done = (f32[3,3,256,256]{3,2,1,0:T(8,128)}, f32[3,256,256]{2,1,0:T(8,128)}, f32[3,256,256]{2,1,0:T(8,128)}) async-done(((f32[3,3,256,256]{3,2,1,0:T(8,128)}, f32[3,256,256]{2,1,0:T(8,128)}, f32[3,256,256]{2,1,0:T(8,128)}), (f32[3,3,256,256]{3,2,1,0:T(8,128)}, f32[3,256,256]{2,1,0:T(8,128)}, f32[3,256,256]{2,1,0:T(8,128)})) %all-reduce.7.cloned.1.call-update) | async-done | bytes 3932176 | tf_op jit(solution)/shard_map/psum | solution.py:215
  390.5 3.4 broadcast_multiply_fusion
  (128 shorter events, 41.9 us)
Async XLA Ops:
  7.2 12.8 %copy-start.3 = (bf16[1,16,1,64,256]{4,3,2,1,0:T(8,128)(2,1)S(1)}, bf16[1,16,1,64,256]{4,3,2,1,0:T(8,128)(2,1)}, u32[]{:S(2)}) copy-start(bf16[1,16,1,64,256]{4,3,2,1,0:T(8,128)(2,1)} %param.13) | copy-start | bytes 1572868
  7.2 12.8 %copy-start.17 = (bf16[3,256,256]{2,1,0:T(8,128)(2,1)S(1)}, bf16[3,256,256]{2,1,0:T(8,128)(2,1)}, u32[]{:S(2)}) copy-start(bf16[3,256,256]{2,1,0:T(8,128)(2,1)} %param.12) | copy-start | bytes 1179652
  11.2 31.1 %copy-start = (bf16[1,4,8,64,256]{4,3,2,1,0:T(8,128)(2,1)}, bf16[1,4,8,64,256]{4,3,2,1,0:T(8,128)(2,1)S(1)}, u32[]{:S(2)}) copy-start(bf16[1,4,8,64,256]{4,3,2,1,0:T(8,128)(2,1)S(1)} %fusion.5) | copy-start | bytes 3145732
  12.0 24.0 %collective-permute-start = (bf16[1,4,1,64,256]{4,3,2,1,0:T(8,128)(2,1)}, bf16[1,4,1,64,256]{4,3,2,1,0:T(8,128)(2,1)S(1)}, u32[]{:S(2)}, u32[]{:S(2)}) collective-permute-start(bf16[1,4,1,64,256]{4,3,2,1,0:T(8,128)(2,1)} %get-tuple-element.42), channel_id=1, source_target_pairs={{0,2},{2,4},{4,6},{6,8},{8,10},{10,12},{12,14},{14,16},{16,18},{18... | collective-permute-start | bytes 393224 | tf_op jit(solution)/shard_map/ppermute | solution.py:15
  15.5 20.6 %collective-permute-start.1 = (bf16[1,4,1,64,256]{4,3,2,1,0:T(8,128)(2,1)}, bf16[1,4,1,64,256]{4,3,2,1,0:T(8,128)(2,1)S(1)}, u32[]{:S(2)}, u32[]{:S(2)}) collective-permute-start(bf16[1,4,1,64,256]{4,3,2,1,0:T(8,128)(2,1)} %get-tuple-element.43), channel_id=1, source_target_pairs={{2,0},{4,2},{6,4},{8,6},{10,8},{12,10},{14,12},{16,14},{18,16},{20... | collective-permute-start | bytes 393224 | tf_op jit(solution)/shard_map/ppermute | solution.py:16
  20.7 9.6 %copy-start.14 = (bf16[3,3,256,256]{3,2,1,0:T(8,128)(2,1)S(1)}, bf16[3,3,256,256]{3,2,1,0:T(8,128)(2,1)}, u32[]{:S(2)}) copy-start(bf16[3,3,256,256]{3,2,1,0:T(8,128)(2,1)} %param.10) | copy-start | bytes 3538948
  21.8 27.7 %all-to-all-start.1 = ((bf16[1,16,1,64,256]{4,3,2,0,1:T(8,128)(2,1)}), bf16[1,16,1,64,256]{4,3,2,0,1:T(8,128)(2,1)S(1)}, u32[]{:S(2)}, u32[]{:S(2)}) async-start(bf16[1,16,1,64,256]{4,3,2,0,1:T(8,128)(2,1)} %fusion.23), calls=%async_computation.1 | async-start | bytes 1048576 | tf_op jit(solution)/shard_map/all_to_all | solution.py:201
  33.6 3.3 copy-start.15
  36.1 6.2 %copy-start.29 = (bf16[1,4,1,64,256]{4,3,2,1,0:T(8,128)(2,1)}, bf16[1,4,1,64,256]{4,3,2,1,0:T(8,128)(2,1)S(1)}, u32[]{:S(2)}) copy-start(bf16[1,4,1,64,256]{4,3,2,1,0:T(8,128)(2,1)S(1)} %collective-permute-done) | copy-start | bytes 393220
  36.1 2.6 copy-start.27
  47.7 5.2 %copy-start.19 = (bf16[3,256,256]{2,1,0:T(8,128)(2,1)S(1)}, bf16[3,256,256]{2,1,0:T(8,128)(2,1)}, u32[]{:S(2)}) copy-start(bf16[3,256,256]{2,1,0:T(8,128)(2,1)} %param.11) | copy-start | bytes 1179652
  50.3 11.2 %copy-start.13 = (f32[4,8,64,256]{3,2,1,0:T(8,128)S(1)}, f32[4,8,64,256]{3,2,1,0:T(8,128)}, u32[]{:S(2)}) copy-start(f32[4,8,64,256]{3,2,1,0:T(8,128)} %fusion.49) | copy-start | bytes 6291460
  51.6 9.1 %collective-permute-start.3 = (bf16[1,1,8,64,256]{4,3,2,1,0:T(8,128)(2,1)S(1)}, bf16[1,1,8,64,256]{4,3,2,1,0:T(8,128)(2,1)S(1)}, u32[]{:S(2)}, u32[]{:S(2)}) collective-permute-start(bf16[1,1,8,64,256]{4,3,2,1,0:T(8,128)(2,1)S(1)} %get-tuple-element.47), channel_id=1, source_target_pairs={{32,0},{64,32},{96,64},{128,96},{160,128},{192,160},{224,192},{33,... | collective-permute-start | bytes 786440 | tf_op jit(solution)/shard_map/ppermute | solution.py:24
  52.9 8.7 %copy-start.12 = (f32[4,8,64,256]{3,2,1,0:T(8,128)S(1)}, f32[4,8,64,256]{3,2,1,0:T(8,128)}, u32[]{:S(2)}) copy-start(f32[4,8,64,256]{3,2,1,0:T(8,128)} %fusion.48) | copy-start | bytes 6291460
  53.3 8.3 %copy-start.11 = (f32[4,8,64,256]{3,2,1,0:T(8,128)S(1)}, f32[4,8,64,256]{3,2,1,0:T(8,128)}, u32[]{:S(2)}) copy-start(f32[4,8,64,256]{3,2,1,0:T(8,128)} %fusion.47) | copy-start | bytes 6291460
  61.3 2.6 copy-start.1
  61.3 3.3 copy-start.7
  61.3 3.3 copy-start.28
  71.3 4.3 %copy-start.20 = (bf16[3,256,256]{2,1,0:T(8,128)(2,1)S(1)}, bf16[3,256,256]{2,1,0:T(8,128)(2,1)}, u32[]{:S(2)}) copy-start(bf16[3,256,256]{2,1,0:T(8,128)(2,1)} %param.11) | copy-start | bytes 1179652
  71.8 12.3 %copy-start.16 = (bf16[3,3,256,256]{3,2,1,0:T(8,128)(2,1)S(1)}, bf16[3,3,256,256]{3,2,1,0:T(8,128)(2,1)}, u32[]{:S(2)}) copy-start(bf16[3,3,256,256]{3,2,1,0:T(8,128)(2,1)} %reverse_bitcast_fusion) | copy-start | bytes 3538948
  71.9 27.2 %collective-permute-start.2 = (bf16[1,1,8,64,256]{4,3,2,1,0:T(8,128)(2,1)S(1)}, bf16[1,1,8,64,256]{4,3,2,1,0:T(8,128)(2,1)S(1)}, u32[]{:S(2)}, u32[]{:S(2)}) collective-permute-start(bf16[1,1,8,64,256]{4,3,2,1,0:T(8,128)(2,1)S(1)} %slice.255), channel_id=1, source_target_pairs={{0,32},{32,64},{64,96},{96,128},{128,160},{160,192},{192,224},{1,3... | collective-permute-start | bytes 786440 | tf_op jit(solution)/shard_map/ppermute | solution.py:24
  76.0 15.1 %collective-permute-start.4 = (bf16[1,4,1,64,256]{4,3,2,1,0:T(8,128)(2,1)S(1)}, bf16[1,4,1,64,256]{4,3,2,1,0:T(8,128)(2,1)S(1)}, u32[]{:S(2)}, u32[]{:S(2)}) collective-permute-start(bf16[1,4,1,64,256]{4,3,2,1,0:T(8,128)(2,1)S(1)} %get-tuple-element.40), channel_id=1, source_target_pairs={{0,2},{2,4},{4,6},{6,8},{8,10},{10,12},{12,14},{14,16},{16,18},{18... | collective-permute-start | bytes 393224 | tf_op jit(solution)/shard_map/ppermute | solution.py:15
  77.9 13.2 %collective-permute-start.5 = (bf16[1,4,1,64,256]{4,3,2,1,0:T(8,128)(2,1)S(1)}, bf16[1,4,1,64,256]{4,3,2,1,0:T(8,128)(2,1)S(1)}, u32[]{:S(2)}, u32[]{:S(2)}) collective-permute-start(bf16[1,4,1,64,256]{4,3,2,1,0:T(8,128)(2,1)S(1)} %get-tuple-element.41), channel_id=1, source_target_pairs={{2,0},{4,2},{6,4},{8,6},{10,8},{12,10},{14,12},{16,14},{18,16},{20... | collective-permute-start | bytes 393224 | tf_op jit(solution)/shard_map/ppermute | solution.py:16
  100.6 20.6 %all-to-all-start = ((bf16[1,2,8,64,256]{4,3,1,0,2:T(8,128)(2,1)}), bf16[1,2,8,64,256]{4,3,1,0,2:T(8,128)(2,1)}, u32[]{:S(2)}, u32[]{:S(2)}) async-start(bf16[1,2,8,64,256]{4,3,1,0,2:T(8,128)(2,1)} %copy.41), calls=%async_computation | async-start | bytes 1048576 | tf_op jit(solution)/shard_map/all_to_all | solution.py:198
  106.4 284.1 %all-reduce.7.cloned.1.call-start = ((), (), s32[]{:S(2)}) async-start(), calls=%async_computation.2 | async-start | bytes 7864320 | tf_op jit(solution)/shard_map/psum | solution.py:215
  111.9 2.7 copy-start.24
  114.6 6.6 %copy-start.4 = (bf16[1,16,1,64,256]{4,3,2,1,0:T(8,128)(2,1)S(1)}, bf16[1,16,1,64,256]{4,3,2,1,0:T(8,128)(2,1)}, u32[]{:S(2)}) copy-start(bf16[1,16,1,64,256]{4,3,2,1,0:T(8,128)(2,1)} %param.13) | copy-start | bytes 1572868
  122.5 2.8 copy-start.21
  122.6 2.8 copy-start.22
  208.2 2.9 copy-start.18
  390.5 3.4 copy-start.26
  390.5 4.3 %copy-start.25 = (f32[3,256,256]{2,1,0:T(8,128)S(1)}, f32[3,256,256]{2,1,0:T(8,128)}, u32[]{:S(2)}) copy-start(f32[3,256,256]{2,1,0:T(8,128)} %get-tuple-element.33) | copy-start | bytes 2359300
  (10 other events, 16.2 us)
Sparse Core Ops, SparseCore 0:
  126.8 263.6 all-reduce.6
where the time goes:
time: 404 us; the launch traced here: 403 us
  waiting for transfers between devices  188 us (47%)
  blocking collectives  71.9 us (18%)
  matrix products  62.2 us (15%)
  starting transfers between devices  35.4 us (9%)
  other arithmetic  16.8 us (4%)
  between operations  15.3 us (4%)
  local copies, waits for them, and re-layouts  13.2 us (3%)
    psum x1, waiting for transfers between devices, on_device(): lax.psum((mix_gradient, temporal_gradient, spatial_gradient, gain_gradien...  174 us
    psum x1, blocking collectives, on_device(): lax.psum((mix_gradient, temporal_gradient, spatial_gradient, gain_gradien...  71.9 us
    dot_general x24, matrix products, project(): product = jnp.dot(flat_rows, weight, preferred_element_type=jnp.float32)  48.4 us
    dot_general x15, matrix products, outer_sum(): lax.dot_general(left_rows.reshape(-1, left_rows.shape[-1]), right_rows.re...  10.9 us
    ppermute x2, starting transfers between devices, extended(): after = lax.ppermute(initial, axis, down)  10.7 us
    all_to_all x1, starting transfers between devices, on_device(): lax.all_to_all(regrouped_gradient, 'tm', split_axis=1, concat_axis=2, til...  8.46 us
  transfers between devices with their start and end apart: 9, of which 3 were waited for; matrix products, arithmetic and copies ran while one was open for 15% of the time, Pallas kernels for 0%

commit v1 on v0

--- a/solution.py
+++ b/solution.py
@@ -213,7 +213,8 @@
         normed_gradient, unit_rows, inverse, norm_gain, present
     )
     mix_gradient, temporal_gradient, spatial_gradient, gain_gradient = lax.psum(
-        (mix_gradient, temporal_gradient, spatial_gradient, gain_gradient), ("tm", "height", "cam")
+        lax.psum((mix_gradient, temporal_gradient, spatial_gradient, gain_gradient), "tm"),
+        ("height", "cam"),
     )
     cell_count = (
         video_clip.shape[0]

time: 404 us -> 342 us (0.85)
  waiting for transfers between devices: 188 us -> 127 us
    psum x1, waiting for transfers between devices: 174 us -> 71.2 us  [on_device(): lax.psum((mix_gradient, temporal_gradient, spatial_gradient, gain_gradien...]
    psum x1, blocking collectives: 71.9 us -> 15.5 us  [on_device(): lax.psum((mix_gradient, temporal_gradient, spatial_gradient, gain_gradien...]
    psum x0 -> x1, blocking collectives: none -> 53.3 us  [on_device(): lax.psum(lax.psum((mix_gradient, temporal_gradient, spatial_gradient, gai...]
    psum x0 -> x1, waiting for transfers between devices: none -> 41.1 us  [on_device(): lax.psum(lax.psum((mix_gradient, temporal_gradient, spatial_gradient, gai...]
    dot_general x24, matrix products: 48.4 us -> 43.9 us  [project(): product = jnp.dot(flat_rows, weight, preferred_element_type=jnp.float32)]
  transfers between devices with their start and end apart: 9 -> 10, of which waited for: 3 -> 7; matrix products, arithmetic and copies ran while one was open for 15% -> 18% of each run, Pallas kernels for 0% -> 0%
where the time goes in v1:
time: 342 us; the launch traced here: 340 us
  waiting for transfers between devices  127 us (37%)
  blocking collectives  68.8 us (20%)
  matrix products  58.7 us (17%)
  starting transfers between devices  38.6 us (11%)
  other arithmetic  19.1 us (6%)
  between operations  15.3 us (4%)
  local copies, waits for them, and re-layouts  12.1 us (4%)
    psum x1, waiting for transfers between devices, on_device(): lax.psum((mix_gradient, temporal_gradient, spatial_gradient, gain_gradien...  71.2 us
    psum x1, blocking collectives, on_device(): lax.psum(lax.psum((mix_gradient, temporal_gradient, spatial_gradient, gai...  53.3 us
    dot_general x24, matrix products, project(): product = jnp.dot(flat_rows, weight, preferred_element_type=jnp.float32)  43.9 us
    psum x1, waiting for transfers between devices, on_device(): lax.psum(lax.psum((mix_gradient, temporal_gradient, spatial_gradient, gai...  41.1 us
    psum x1, blocking collectives, on_device(): lax.psum((mix_gradient, temporal_gradient, spatial_gradient, gain_gradien...  15.5 us
    dot_general x15, matrix products, outer_sum(): lax.dot_general(left_rows.reshape(-1, left_rows.shape[-1]), right_rows.re...  12 us
    ppermute x2, starting transfers between devices, extended(): after = lax.ppermute(initial, axis, down)  10.5 us
    all_to_all x1, starting transfers between devices, on_device(): lax.all_to_all(strided, 'tm', split_axis=2, concat_axis=1, tiled=True)  8.9 us
  transfers between devices with their start and end apart: 10, of which 7 were waited for; matrix products, arithmetic and copies ran while one was open for 18% of the time, Pallas kernels for 0%

profile of v1, /device:TPU:2, one launch (start us, length us, event | category | flops | bytes accessed | tf_op | source)
XLA Modules:
  0.0 340.1 jit_solution(17189298792950957436)
XLA Ops:
  11.3 3.5 %collective-permute-start = (bf16[1,4,1,64,256]{4,3,2,1,0:T(8,128)(2,1)S(1)}, bf16[1,4,1,64,256]{4,3,2,1,0:T(8,128)(2,1)S(1)}, u32[]{:S(2)}, u32[]{:S(2)}) collective-permute-start(bf16[1,4,1,64,256]{4,3,2,1,0:T(8,128)(2,1)S(1)} %get-tuple-element.45), channel_id=1, source_target_pairs={{0,2},{2,4},{4,6},{6,8},{8,10},{10,12},{12,14},{14,16},{16,18},{18... | collective-permute-start | bytes 393224 | tf_op jit(solution)/shard_map/ppermute | solution.py:15
  14.8 4.5 %collective-permute-start.1 = (bf16[1,4,1,64,256]{4,3,2,1,0:T(8,128)(2,1)S(1)}, bf16[1,4,1,64,256]{4,3,2,1,0:T(8,128)(2,1)S(1)}, u32[]{:S(2)}, u32[]{:S(2)}) collective-permute-start(bf16[1,4,1,64,256]{4,3,2,1,0:T(8,128)(2,1)S(1)} %get-tuple-element.46), channel_id=1, source_target_pairs={{2,0},{4,2},{6,4},{8,6},{10,8},{12,10},{14,12},{16,14},{18,16},{20... | collective-permute-start | bytes 393224 | tf_op jit(solution)/shard_map/ppermute | solution.py:16
  21.1 8.5 %all-to-all-start.1 = ((bf16[1,16,1,64,256]{4,3,2,0,1:T(8,128)(2,1)}), bf16[1,16,1,64,256]{4,3,2,0,1:T(8,128)(2,1)S(1)}, u32[]{:S(2)}, u32[]{:S(2)}) async-start(bf16[1,16,1,64,256]{4,3,2,0,1:T(8,128)(2,1)} %fusion.23), calls=%async_computation.1 | async-start | bytes 1048576 | tf_op jit(solution)/shard_map/all_to_all | solution.py:201
  29.6 2.7 fusion.42
  33.6 1.8 fusion.44
  35.5 1.8 fusion.45
  37.2 1.8 fusion.46
  39.0 1.8 fusion.51
  40.9 1.8 fusion.47
  44.5 1.8 fusion.49
  50.6 6.9 %collective-permute-done.3 = bf16[1,1,8,64,256]{4,3,2,1,0:T(8,128)(2,1)S(1)} collective-permute-done((bf16[1,1,8,64,256]{4,3,2,1,0:T(8,128)(2,1)S(1)}, bf16[1,1,8,64,256]{4,3,2,1,0:T(8,128)(2,1)S(1)}, u32[]{:S(2)}, u32[]{:S(2)}) %collective-permute-start.3) | collective-permute-done | bytes 262176 | tf_op jit(solution)/shard_map/ppermute | solution.py:24
  61.3 3.2 fusion.14
  70.8 4.0 %collective-permute-start.2 = (bf16[1,1,8,64,256]{4,3,2,1,0:T(8,128)(2,1)S(1)}, bf16[1,1,8,64,256]{4,3,2,1,0:T(8,128)(2,1)S(1)}, u32[]{:S(2)}, u32[]{:S(2)}) collective-permute-start(bf16[1,1,8,64,256]{4,3,2,1,0:T(8,128)(2,1)S(1)} %slice.255), channel_id=1, source_target_pairs={{0,32},{32,64},{64,96},{96,128},{128,160},{160,192},{192,224},{1,3... | collective-permute-start | bytes 786440 | tf_op jit(solution)/shard_map/ppermute | solution.py:24
  80.6 8.9 %all-to-all-start = ((bf16[1,2,8,64,256]{4,3,1,0,2:T(8,128)(2,1)}), bf16[1,2,8,64,256]{4,3,1,0,2:T(8,128)(2,1)S(1)}, u32[]{:S(2)}, u32[]{:S(2)}) async-start(bf16[1,2,8,64,256]{4,3,1,0,2:T(8,128)(2,1)} %copy.41), calls=%async_computation | async-start | bytes 1048576 | tf_op jit(solution)/shard_map/all_to_all | solution.py:198
  90.8 2.1 convolution_bitcast_fusion.8
  92.9 2.1 convolution_bitcast_fusion.9
  96.9 6.9 %all-to-all-done = bf16[1,2,8,64,256]{4,3,1,0,2:T(8,128)(2,1)S(1)} async-done(((bf16[1,2,8,64,256]{4,3,1,0,2:T(8,128)(2,1)}), bf16[1,2,8,64,256]{4,3,1,0,2:T(8,128)(2,1)S(1)}, u32[]{:S(2)}, u32[]{:S(2)}) %all-to-all-start) | async-done | bytes 524320 | tf_op jit(solution)/shard_map/all_to_all | solution.py:198
  106.5 2.4 copy.47
  110.3 1.9 collective-permute-start.4
  112.3 6.0 %collective-permute-start.5 = (bf16[1,4,1,64,256]{4,3,2,1,0:T(8,128)(2,1)S(1)}, bf16[1,4,1,64,256]{4,3,2,1,0:T(8,128)(2,1)S(1)}, u32[]{:S(2)}, u32[]{:S(2)}) collective-permute-start(bf16[1,4,1,64,256]{4,3,2,1,0:T(8,128)(2,1)S(1)} %get-tuple-element.44), channel_id=1, source_target_pairs={{2,0},{4,2},{6,4},{8,6},{10,8},{12,10},{14,12},{16,14},{18,16},{20... | collective-permute-start | bytes 393224 | tf_op jit(solution)/shard_map/ppermute | solution.py:16
  118.3 1.9 fusion.77
  121.6 1.8 fusion.35
  123.4 1.8 fusion.26
  125.2 1.8 fusion.30
  130.5 1.8 fusion.33
  134.0 71.2 %all-reduce.11.cloned.1.call-done = (f32[3,3,256,256]{3,2,1,0:T(8,128)}, f32[3,256,256]{2,1,0:T(8,128)}, f32[3,256,256]{2,1,0:T(8,128)}) async-done(((f32[3,3,256,256]{3,2,1,0:T(8,128)}, f32[3,256,256]{2,1,0:T(8,128)}, f32[3,256,256]{2,1,0:T(8,128)}), (f32[3,3,256,256]{3,2,1,0:T(8,128)}, f32[3,256,256]{2,1,0:T(8,128)}, f32[3,256,256]{2,1,0:T(8,128)})) %all-reduce.11.cloned.1.call-update) | async-done | bytes 3932176 | tf_op jit(solution)/shard_map/psum | solution.py:216
  205.3 7.6 %fusion.11 = (f32[256]{0:T(256)S(1)}, f32[4,8,64]{2,1,0:T(8,128)S(1)}, f32[4,8,64,256]{3,2,1,0:T(8,128)}) fusion(f32[4,8,64]{2,1,0:T(8,128)S(1)} %add_rsqrt_fusion, bf16[1,4,8,64,256]{4,3,2,1,0:T(8,128)(2,1)S(1)} %copy-done.2, pred[4]{0:T(512)(128)(4,1)S(1)} %copy-done.34, f32[256]{0:T(256)S(1)} %copy-done.32, f32[4,8,64,256]{3,2,1,0:T(8,128)} %fusion.26, ...), kind=kOutput, calls=%fused_computation.16 | convolution fusion | flops 277346048 | bytes 21252100 | tf_op jit(solution)/shard_map/dot_general | solution.py:29
  212.8 15.5 %psum.62 = f32[256]{0:T(256)S(1)} all-reduce(f32[256]{0:T(256)S(1)} %get-tuple-element.30), channel_id=1, replica_groups=mesh['tm'=8,'height'=16,'cam'=2] {'tm'}, use_global_device_ids=true, to_apply=%region_9.10 | all-reduce | flops 256 | bytes 2048 | tf_op jit(solution)/shard_map/psum | solution.py:216
  228.3 53.3 %psum.63 = f32[256]{0:T(256)S(1)} all-reduce(f32[256]{0:T(256)S(1)} %psum.62), channel_id=1, replica_groups=mesh['tm'=8,'height'=16,'cam'=2] {'height','cam'}, use_global_device_ids=true, to_apply=%region_10.11 | all-reduce | flops 256 | bytes 2048 | tf_op jit(solution)/shard_map/psum | solution.py:215
  282.2 2.9 fusion.10
  286.8 41.1 %all-reduce.9.cloned.1.call-done = (f32[3,3,256,256]{3,2,1,0:T(8,128)}, f32[3,256,256]{2,1,0:T(8,128)}, f32[3,256,256]{2,1,0:T(8,128)}) async-done(((f32[3,3,256,256]{3,2,1,0:T(8,128)}, f32[3,256,256]{2,1,0:T(8,128)}, f32[3,256,256]{2,1,0:T(8,128)}), (f32[3,3,256,256]{3,2,1,0:T(8,128)}, f32[3,256,256]{2,1,0:T(8,128)}, f32[3,256,256]{2,1,0:T(8,128)})) %all-reduce.9.cloned.1.call-update) | async-done | bytes 3932176 | tf_op jit(solution)/shard_map/psum | solution.py:215
  327.9 3.4 broadcast_multiply_fusion
  (136 shorter events, 46.4 us)
Async XLA Ops:
  7.2 12.1 %copy-start.3 = (bf16[1,16,1,64,256]{4,3,2,1,0:T(8,128)(2,1)S(1)}, bf16[1,16,1,64,256]{4,3,2,1,0:T(8,128)(2,1)}, u32[]{:S(2)}) copy-start(bf16[1,16,1,64,256]{4,3,2,1,0:T(8,128)(2,1)} %param.13) | copy-start | bytes 1572868
  7.2 12.1 %copy-start.18 = (bf16[3,256,256]{2,1,0:T(8,128)(2,1)S(1)}, bf16[3,256,256]{2,1,0:T(8,128)(2,1)}, u32[]{:S(2)}) copy-start(bf16[3,256,256]{2,1,0:T(8,128)(2,1)} %param.12) | copy-start | bytes 1179652
  11.3 27.8 %copy-start = (bf16[1,4,8,64,256]{4,3,2,1,0:T(8,128)(2,1)}, bf16[1,4,8,64,256]{4,3,2,1,0:T(8,128)(2,1)S(1)}, u32[]{:S(2)}) copy-start(bf16[1,4,8,64,256]{4,3,2,1,0:T(8,128)(2,1)S(1)} %fusion.5) | copy-start | bytes 3145732
  11.3 21.0 %collective-permute-start = (bf16[1,4,1,64,256]{4,3,2,1,0:T(8,128)(2,1)S(1)}, bf16[1,4,1,64,256]{4,3,2,1,0:T(8,128)(2,1)S(1)}, u32[]{:S(2)}, u32[]{:S(2)}) collective-permute-start(bf16[1,4,1,64,256]{4,3,2,1,0:T(8,128)(2,1)S(1)} %get-tuple-element.45), channel_id=1, source_target_pairs={{0,2},{2,4},{4,6},{6,8},{8,10},{10,12},{12,14},{14,16},{16,18},{18... | collective-permute-start | bytes 393224 | tf_op jit(solution)/shard_map/ppermute | solution.py:15
  14.8 17.5 %collective-permute-start.1 = (bf16[1,4,1,64,256]{4,3,2,1,0:T(8,128)(2,1)S(1)}, bf16[1,4,1,64,256]{4,3,2,1,0:T(8,128)(2,1)S(1)}, u32[]{:S(2)}, u32[]{:S(2)}) collective-permute-start(bf16[1,4,1,64,256]{4,3,2,1,0:T(8,128)(2,1)S(1)} %get-tuple-element.46), channel_id=1, source_target_pairs={{2,0},{4,2},{6,4},{8,6},{10,8},{12,10},{14,12},{16,14},{18,16},{20... | collective-permute-start | bytes 393224 | tf_op jit(solution)/shard_map/ppermute | solution.py:16
  21.1 25.4 %all-to-all-start.1 = ((bf16[1,16,1,64,256]{4,3,2,0,1:T(8,128)(2,1)}), bf16[1,16,1,64,256]{4,3,2,0,1:T(8,128)(2,1)S(1)}, u32[]{:S(2)}, u32[]{:S(2)}) async-start(bf16[1,16,1,64,256]{4,3,2,0,1:T(8,128)(2,1)} %fusion.23), calls=%async_computation.1 | async-start | bytes 1048576 | tf_op jit(solution)/shard_map/all_to_all | solution.py:201
  32.3 6.7 %copy-start.29 = (bf16[1,4,1,64,256]{4,3,2,1,0:T(8,128)(2,1)}, bf16[1,4,1,64,256]{4,3,2,1,0:T(8,128)(2,1)S(1)}, u32[]{:S(2)}) copy-start(bf16[1,4,1,64,256]{4,3,2,1,0:T(8,128)(2,1)S(1)} %collective-permute-done) | copy-start | bytes 393220
  32.3 3.2 copy-start.27
  44.5 5.4 %copy-start.20 = (bf16[3,256,256]{2,1,0:T(8,128)(2,1)S(1)}, bf16[3,256,256]{2,1,0:T(8,128)(2,1)}, u32[]{:S(2)}) copy-start(bf16[3,256,256]{2,1,0:T(8,128)(2,1)} %param.11) | copy-start | bytes 1179652
  47.3 11.0 %copy-start.13 = (f32[4,8,64,256]{3,2,1,0:T(8,128)S(1)}, f32[4,8,64,256]{3,2,1,0:T(8,128)}, u32[]{:S(2)}) copy-start(f32[4,8,64,256]{3,2,1,0:T(8,128)} %fusion.49) | copy-start | bytes 6291460
  48.6 8.8 %collective-permute-start.3 = (bf16[1,1,8,64,256]{4,3,2,1,0:T(8,128)(2,1)S(1)}, bf16[1,1,8,64,256]{4,3,2,1,0:T(8,128)(2,1)S(1)}, u32[]{:S(2)}, u32[]{:S(2)}) collective-permute-start(bf16[1,1,8,64,256]{4,3,2,1,0:T(8,128)(2,1)S(1)} %get-tuple-element.50), channel_id=1, source_target_pairs={{32,0},{64,32},{96,64},{128,96},{160,128},{192,160},{224,192},{33,... | collective-permute-start | bytes 786440 | tf_op jit(solution)/shard_map/ppermute | solution.py:24
  49.9 8.4 %copy-start.12 = (f32[4,8,64,256]{3,2,1,0:T(8,128)S(1)}, f32[4,8,64,256]{3,2,1,0:T(8,128)}, u32[]{:S(2)}) copy-start(f32[4,8,64,256]{3,2,1,0:T(8,128)} %fusion.48) | copy-start | bytes 6291460
  50.2 8.1 %copy-start.11 = (f32[4,8,64,256]{3,2,1,0:T(8,128)S(1)}, f32[4,8,64,256]{3,2,1,0:T(8,128)}, u32[]{:S(2)}) copy-start(f32[4,8,64,256]{3,2,1,0:T(8,128)} %fusion.47) | copy-start | bytes 6291460
  58.0 3.3 copy-start.7
  58.0 3.3 copy-start.28
  70.8 4.3 %copy-start.30 = (bf16[1,4,1,64,256]{4,3,2,1,0:T(8,128)(2,1)S(1)}, bf16[1,4,1,64,256]{4,3,2,1,0:T(8,128)(2,1)}, u32[]{:S(2)}) copy-start(bf16[1,4,1,64,256]{4,3,2,1,0:T(8,128)(2,1)} %copy-done.29) | copy-start | bytes 393220
  70.8 7.7 %collective-permute-start.2 = (bf16[1,1,8,64,256]{4,3,2,1,0:T(8,128)(2,1)S(1)}, bf16[1,1,8,64,256]{4,3,2,1,0:T(8,128)(2,1)S(1)}, u32[]{:S(2)}, u32[]{:S(2)}) collective-permute-start(bf16[1,1,8,64,256]{4,3,2,1,0:T(8,128)(2,1)S(1)} %slice.255), channel_id=1, source_target_pairs={{0,32},{32,64},{64,96},{96,128},{128,160},{160,192},{192,224},{1,3... | collective-permute-start | bytes 786440 | tf_op jit(solution)/shard_map/ppermute | solution.py:24
  79.8 9.8 %copy-start.31 = (f32[1,256,256]{2,1,0:T(8,128)S(1)}, f32[1,256,256]{2,1,0:T(8,128)}, u32[]{:S(2)}) copy-start(f32[1,256,256]{2,1,0:T(8,128)} %convolution_bitcast_fusion.11) | copy-start | bytes 786436
  80.6 23.2 %all-to-all-start = ((bf16[1,2,8,64,256]{4,3,1,0,2:T(8,128)(2,1)}), bf16[1,2,8,64,256]{4,3,1,0,2:T(8,128)(2,1)S(1)}, u32[]{:S(2)}, u32[]{:S(2)}) async-start(bf16[1,2,8,64,256]{4,3,1,0,2:T(8,128)(2,1)} %copy.41), calls=%async_computation | async-start | bytes 1048576 | tf_op jit(solution)/shard_map/all_to_all | solution.py:198
  89.5 115.7 %all-reduce.11.cloned.1.call-start = ((), (), s32[]{:S(2)}) async-start(), calls=%async_computation.3 | async-start | bytes 7864320 | tf_op jit(solution)/shard_map/psum | solution.py:216
  89.6 5.4 %copy-start.16 = (f32[1,3,256,256]{3,2,1,0:T(8,128)S(1)}, f32[1,3,256,256]{3,2,1,0:T(8,128)}, u32[]{:S(2)}) copy-start(f32[1,3,256,256]{3,2,1,0:T(8,128)} %get-tuple-element.52) | copy-start | bytes 2359300
  89.6 5.4 %copy-start.17 = (f32[1,3,256,256]{3,2,1,0:T(8,128)S(1)}, f32[1,3,256,256]{3,2,1,0:T(8,128)}, u32[]{:S(2)}) copy-start(f32[1,3,256,256]{3,2,1,0:T(8,128)} %get-tuple-element.53) | copy-start | bytes 2359300
  96.6 7.3 %copy-start.4 = (bf16[1,16,1,64,256]{4,3,2,1,0:T(8,128)(2,1)S(1)}, bf16[1,16,1,64,256]{4,3,2,1,0:T(8,128)(2,1)}, u32[]{:S(2)}) copy-start(bf16[1,16,1,64,256]{4,3,2,1,0:T(8,128)(2,1)} %param.13) | copy-start | bytes 1572868
  106.5 221.4 %all-reduce.9.cloned.1.call-start = ((), (), s32[]{:S(2)}) async-start(), calls=%async_computation.2 | async-start | bytes 7864320 | tf_op jit(solution)/shard_map/psum | solution.py:215
  110.3 22.0 %copy-start.15 = (bf16[3,3,256,256]{3,2,1,0:T(8,128)(2,1)}, bf16[3,3,256,256]{3,2,1,0:T(8,128)(2,1)S(1)}, u32[]{:S(2)}) copy-start(bf16[3,3,256,256]{3,2,1,0:T(8,128)(2,1)S(1)} %reverse_bitcast_fusion) | copy-start | bytes 3538948
  110.3 9.8 %collective-permute-start.4 = (bf16[1,4,1,64,256]{4,3,2,1,0:T(8,128)(2,1)S(1)}, bf16[1,4,1,64,256]{4,3,2,1,0:T(8,128)(2,1)S(1)}, u32[]{:S(2)}, u32[]{:S(2)}) collective-permute-start(bf16[1,4,1,64,256]{4,3,2,1,0:T(8,128)(2,1)S(1)} %get-tuple-element.43), channel_id=1, source_target_pairs={{0,2},{2,4},{4,6},{6,8},{8,10},{10,12},{12,14},{14,16},{16,18},{18... | collective-permute-start | bytes 393224 | tf_op jit(solution)/shard_map/ppermute | solution.py:15
  112.3 8.5 %collective-permute-start.5 = (bf16[1,4,1,64,256]{4,3,2,1,0:T(8,128)(2,1)S(1)}, bf16[1,4,1,64,256]{4,3,2,1,0:T(8,128)(2,1)S(1)}, u32[]{:S(2)}, u32[]{:S(2)}) collective-permute-start(bf16[1,4,1,64,256]{4,3,2,1,0:T(8,128)(2,1)S(1)} %get-tuple-element.44), channel_id=1, source_target_pairs={{2,0},{4,2},{6,4},{8,6},{10,8},{12,10},{14,12},{16,14},{18,16},{20... | collective-permute-start | bytes 393224 | tf_op jit(solution)/shard_map/ppermute | solution.py:16
  134.0 71.3 %copy-start.2 = (bf16[1,4,8,64,256]{4,3,2,1,0:T(8,128)(2,1)S(1)}, bf16[1,4,8,64,256]{4,3,2,1,0:T(8,128)(2,1)}, u32[]{:S(2)}) copy-start(bf16[1,4,8,64,256]{4,3,2,1,0:T(8,128)(2,1)} %param.7) | copy-start | bytes 3145732
  134.0 71.3 %copy-start.32 = (f32[256]{0:T(256)S(1)}, f32[256]{0:T(256)}, u32[]{:S(2)}) copy-start(f32[256]{0:T(256)} %param.9) | copy-start | bytes 3076
  134.0 71.3 %copy-start.34 = (pred[4]{0:T(512)(128)(4,1)S(1)}, pred[4]{0:T(512)(128)(4,1)}, u32[]{:S(2)}) copy-start(pred[4]{0:T(512)(128)(4,1)} %copy-done.33) | copy-start | bytes 16
  327.9 3.4 copy-start.26
  327.9 4.3 %copy-start.25 = (f32[3,256,256]{2,1,0:T(8,128)S(1)}, f32[3,256,256]{2,1,0:T(8,128)}, u32[]{:S(2)}) copy-start(f32[3,256,256]{2,1,0:T(8,128)} %get-tuple-element.33) | copy-start | bytes 2359300
  (13 other events, 22.9 us)
Sparse Core Ops, SparseCore 0:
  106.6 98.5 all-reduce.10
  208.9 118.9 all-reduce.8
